TPU v7x, 32 devices: a whole 2x2x4 slice. The times are simulated.
32 devices in a mesh: batch: 4 (over y, x), seq: 8 (over z, core).
Axes of the slice: x: 2, y: 2, z: 4, core: 2. Of those that a mesh axis runs over, the one named last changes fastest.
Arguments:
- hidden: float32 [8192, 1024], P(('batch', 'seq')), may hold values from -6 to 6
- cotangent: float32 [8192, 1024], P(('batch', 'seq')), may hold values from -6 to 6
- norm_gain: bfloat16 [2, 1024], P(None, ('batch', 'seq')), may hold values from 0.099609375 to 1.8984375
- in_proj: bfloat16 [2, 1024, 4384], P(None, ('batch', 'seq')), may hold values from -0.1875 to 0.1875
- conv_weight: bfloat16 [2, 4, 2304], P(None, None, ('batch', 'seq')), may hold values from -3 to 3
- conv_bias: bfloat16 [2, 2304], P(None, ('batch', 'seq')), may hold values from -3 to 3
- dt_bias: float32 [2, 32], P(None, 'seq'), may hold values from -6 to -1
- a_log: float32 [2, 32], P(None, 'seq'), may hold values from -1.5 to 2.5
- d_skip: float32 [2, 32], P(None, 'seq'), may hold values from 0.5 to 1.5
- gate_gain: bfloat16 [2, 2048], P(None, ('batch', 'seq')), may hold values from 0.099609375 to 1.8984375
- out_proj: bfloat16 [2, 2048, 1024], P(None, ('batch', 'seq')), may hold values from -0.125 to 0.125
Outputs:
- output: float32 [8192, 1024], P(('batch', 'seq'))
- grad_hidden: float32 [8192, 1024], P(('batch', 'seq'))
- grad_norm_gain: float32 [2, 1024], P(None, ('batch', 'seq'))
- grad_in_proj: float32 [2, 1024, 4384], P(None, ('batch', 'seq'))
- grad_conv_weight: float32 [2, 4, 2304], P(None, None, ('batch', 'seq'))
- grad_conv_bias: float32 [2, 2304], P(None, ('batch', 'seq'))
- grad_dt_bias: float32 [2, 32], P(None, 'seq')
- grad_a_log: float32 [2, 32], P(None, 'seq')
- grad_d_skip: float32 [2, 32], P(None, 'seq')
- grad_gate_gain: float32 [2, 2048], P(None, ('batch', 'seq'))
- grad_out_proj: float32 [2, 2048, 1024], P(None, ('batch', 'seq'))
All inputs are finite; a program needn't handle non-finite values.
Results may differ from a plain program's by a relative error of at most 0.023.
Values may be sent and summed in bfloat16 or wider, within the bound.
No kernel may reach another device: no remote copies, remote signals or barrier semaphores. Data moves between devices by JAX's collectives and lax.ppermute only.
A program may use at most 320 MiB of HBM per device.

v0:
```python
import jax
import jax.numpy as jnp
from jax import lax
from jax.sharding import PartitionSpec as P

STATE = 128
SPAN = 256
SEQLEN = 2048
INNER = 2048
EPS = 1e-05
HIGHEST = lax.Precision.HIGHEST


def row_norm(rows, gain):
    factor = lax.rsqrt(jnp.mean(rows * rows, axis=-1, keepdims=True) + EPS)
    return rows * factor * gain


def causal_conv(signal, kernel, offset):
    taps = kernel.shape[0]
    length = signal.shape[0]
    padded = jnp.pad(signal, ((taps - 1, 0), (0, 0)))
    summed = offset + jnp.zeros_like(signal)
    for k in range(taps):
        summed = summed + kernel[k] * padded[k : k + length]
    return jax.nn.silu(summed)


def state_space(inputs, step_size, decay_rate, in_coef, out_coef):
    length, head_count, head_width = inputs.shape
    state_dim = in_coef.shape[1]
    blocks = length // SPAN
    blocked = inputs.reshape(blocks, SPAN, head_count, head_width)
    step_blk = step_size.reshape(blocks, SPAN, head_count)
    in_blk = in_coef.reshape(blocks, SPAN, state_dim)
    out_blk = out_coef.reshape(blocks, SPAN, state_dim)
    running = jnp.cumsum(step_blk * decay_rate, axis=1)
    run_heads = jnp.transpose(running, (0, 2, 1))
    step_heads = jnp.transpose(step_blk, (0, 2, 1))
    position = jnp.arange(SPAN)
    causal = (position[:, None] >= position[None, :])[None, None, :, :]
    spread = run_heads[:, :, :, None] - run_heads[:, :, None, :]
    decays = jnp.where(causal, jnp.exp(jnp.where(causal, spread, 0.0)), 0.0)
    scores = jnp.einsum("ctn,csn->cts", out_blk, in_blk, precision=HIGHEST)
    mixing = scores[:, None, :, :] * decays * step_heads[:, :, None, :]
    within = jnp.einsum("chts,cshp->cthp", mixing, blocked, precision=HIGHEST)
    to_end = jnp.exp(running[:, -1:, :] - running) * step_blk
    weighted = blocked * to_end[:, :, :, None]
    states = jnp.einsum("csn,cshp->chpn", in_blk, weighted, precision=HIGHEST)
    block_decay = jnp.exp(running[:, -1, :])

    def advance(carried, element):
        fresh, factor = element
        return (carried * factor[:, None, None] + fresh, carried)

    initial = jnp.zeros((head_count, head_width, state_dim), jnp.float32)
    _, entering = lax.scan(advance, initial, (states, block_decay))
    from_past = jnp.einsum("ctn,chpn->cthp", out_blk, entering, precision=HIGHEST)
    from_past = from_past * jnp.exp(running)[:, :, :, None]
    return (within + from_past).reshape(length, head_count, head_width)


def mixer(conv_x, conv_coef, gate_in, dt_raw, dt_shift, log_rate, skip_coef):
    length = conv_x.shape[0]
    head_count = dt_raw.shape[1]
    inputs = conv_x.reshape(length, head_count, -1)
    step_size = jax.nn.softplus(dt_raw + dt_shift)
    decay_rate = -jnp.exp(log_rate)
    half = conv_coef.shape[1] // 2
    mixed = state_space(inputs, step_size, decay_rate, conv_coef[:, :half], conv_coef[:, half:])
    mixed = mixed + skip_coef[None, :, None] * inputs
    return mixed.reshape(length, -1) * jax.nn.silu(gate_in)


def contract_rows(left, right):
    return lax.dot_general(
        left, right, (((0,), (0,)), ((), ())), preferred_element_type=jnp.float32
    )


def contract_cols(left, right):
    return lax.dot_general(
        left, right, (((1,), (1,)), ((), ())), preferred_element_type=jnp.float32
    )


def local(
    hidden,
    cotangent,
    norm_gain,
    in_proj,
    conv_weight,
    conv_bias,
    dt_bias,
    a_log,
    d_skip,
    gate_gain,
    out_proj,
):
    layers = in_proj.shape[0]
    pieces = lax.axis_size("seq")
    piece_index = lax.axis_index("seq")
    local_inner = INNER // pieces
    col_start = piece_index * local_inner
    conv_batch = jax.vmap(causal_conv, in_axes=(0, None, None))
    group_mix = jax.vmap(mixer, in_axes=(0, 0, 0, 0, None, None, None))
    stream = hidden
    stored = []
    for layer_idx in range(layers):
        gathered = (
            lax.all_gather(norm_gain[layer_idx], ("batch", "seq"), axis=0, tiled=True),
            lax.all_gather(in_proj[layer_idx], ("batch", "seq"), axis=0, tiled=True),
            lax.all_gather(conv_weight[layer_idx], ("batch", "seq"), axis=1, tiled=True),
            lax.all_gather(conv_bias[layer_idx], ("batch", "seq"), axis=0, tiled=True),
            lax.all_gather(gate_gain[layer_idx], ("batch", "seq"), axis=0, tiled=True),
            lax.all_gather(out_proj[layer_idx], ("batch", "seq"), axis=0, tiled=True),
        )
        n_gain, w_in, c_weight, c_bias, g_gain, w_out = gathered
        normed = row_norm(stream, n_gain.astype(jnp.float32)).astype(jnp.bfloat16)
        projected = jnp.dot(normed, w_in, preferred_element_type=jnp.float32).astype(jnp.bfloat16)
        gate_tok = projected[:, :INNER]
        x_tok = projected[:, INNER : 2 * INNER]
        coef_tok = projected[:, 2 * INNER : 2 * INNER + 2 * STATE]
        steps_tok = projected[:, 2 * INNER + 2 * STATE :]
        x_head, gate_head, steps_head = (
            lax.all_to_all(x_tok, "seq", split_axis=1, concat_axis=0, tiled=True),
            lax.all_to_all(gate_tok, "seq", split_axis=1, concat_axis=0, tiled=True),
            lax.all_to_all(steps_tok, "seq", split_axis=1, concat_axis=0, tiled=True),
        )
        coef_all = lax.all_gather(coef_tok, "seq", axis=0, tiled=True)
        group_rows = x_head.shape[0]
        seq_count = group_rows // SEQLEN
        kernel = jnp.concatenate(
            [lax.dynamic_slice_in_dim(c_weight, col_start, local_inner, 1), c_weight[:, INNER:]],
            axis=1,
        ).astype(jnp.float32)
        offset = jnp.concatenate(
            [lax.dynamic_slice_in_dim(c_bias, col_start, local_inner, 0), c_bias[INNER:]]
        ).astype(jnp.float32)
        signal = (
            jnp.concatenate([x_head, coef_all], axis=1)
            .astype(jnp.float32)
            .reshape(seq_count, SEQLEN, -1)
        )
        conv_out = conv_batch(signal, kernel, offset).astype(jnp.bfloat16)
        mix_args = (
            conv_out[:, :, :local_inner].astype(jnp.float32),
            conv_out[:, :, local_inner:].astype(jnp.float32),
            gate_head.astype(jnp.float32).reshape(seq_count, SEQLEN, -1),
            steps_head.astype(jnp.float32).reshape(seq_count, SEQLEN, -1),
            dt_bias[layer_idx],
            a_log[layer_idx],
            d_skip[layer_idx],
        )
        gated_head = group_mix(*mix_args).reshape(group_rows, -1).astype(jnp.bfloat16)
        gated = lax.all_to_all(gated_head, "seq", split_axis=0, concat_axis=1, tiled=True)
        gnormed = row_norm(gated.astype(jnp.float32), g_gain.astype(jnp.float32)).astype(
            jnp.bfloat16
        )
        stored.append((gathered, stream, normed, signal, kernel, offset, mix_args, gated, gnormed))
        stream = stream + jnp.dot(gnormed, w_out, preferred_element_type=jnp.float32)
    upstream = cotangent
    weight_parts = [None] * layers
    head_parts = [None] * layers
    for layer_idx in reversed(range(layers)):
        gathered, stream_in, normed, signal, kernel, offset, mix_args, gated, gnormed = stored[
            layer_idx
        ]
        gathered = (
            lax.all_gather(norm_gain[layer_idx], ("batch", "seq"), axis=0, tiled=True),
            lax.all_gather(in_proj[layer_idx], ("batch", "seq"), axis=0, tiled=True),
            lax.all_gather(conv_weight[layer_idx], ("batch", "seq"), axis=1, tiled=True),
            lax.all_gather(conv_bias[layer_idx], ("batch", "seq"), axis=0, tiled=True),
            lax.all_gather(gate_gain[layer_idx], ("batch", "seq"), axis=0, tiled=True),
            lax.all_gather(out_proj[layer_idx], ("batch", "seq"), axis=0, tiled=True),
        )
        n_gain, w_in, c_weight, c_bias, g_gain, w_out = gathered
        upstream_b = upstream.astype(jnp.bfloat16)
        grad_out = contract_rows(gnormed, upstream_b)
        d_gnormed = contract_cols(upstream_b, w_out)
        _, pull_gate = jax.vjp(row_norm, gated.astype(jnp.float32), g_gain.astype(jnp.float32))
        d_gated, grad_ggain = pull_gate(d_gnormed)
        d_head = lax.all_to_all(
            d_gated.astype(jnp.bfloat16), "seq", split_axis=1, concat_axis=0, tiled=True
        )
        group_rows = d_head.shape[0]
        seq_count = group_rows // SEQLEN
        _, pull_mix = jax.vjp(group_mix, *mix_args)
        d_convx, d_coef, d_gate, d_steps, grad_shift, grad_rate, grad_skip = pull_mix(
            d_head.astype(jnp.float32).reshape(seq_count, SEQLEN, -1)
        )
        _, pull_conv = jax.vjp(conv_batch, signal, kernel, offset)
        d_signal, grad_kernel, grad_offset = pull_conv(jnp.concatenate([d_convx, d_coef], axis=2))
        d_signal = d_signal.reshape(group_rows, -1)
        d_x_tok, d_gate_tok, d_steps_tok = (
            lax.all_to_all(
                d_signal[:, :local_inner].astype(jnp.bfloat16),
                "seq",
                split_axis=0,
                concat_axis=1,
                tiled=True,
            ),
            lax.all_to_all(
                d_gate.reshape(group_rows, -1).astype(jnp.bfloat16),
                "seq",
                split_axis=0,
                concat_axis=1,
                tiled=True,
            ),
            lax.all_to_all(
                d_steps.reshape(group_rows, -1).astype(jnp.bfloat16),
                "seq",
                split_axis=0,
                concat_axis=1,
                tiled=True,
            ),
        )
        d_coef_tok = lax.psum_scatter(
            d_signal[:, local_inner:].astype(jnp.bfloat16), "seq", scatter_dimension=0, tiled=True
        )
        d_projected = jnp.concatenate([d_gate_tok, d_x_tok, d_coef_tok, d_steps_tok], axis=1)
        grad_in = contract_rows(normed, d_projected)
        d_normed = contract_cols(d_projected, w_in)
        _, pull_norm = jax.vjp(row_norm, stream_in, n_gain.astype(jnp.float32))
        d_stream, grad_ngain = pull_norm(d_normed)
        upstream = upstream + d_stream
        zero_cols = jnp.zeros((grad_kernel.shape[0], INNER), jnp.float32)
        grad_conv_w = jnp.concatenate(
            [
                lax.dynamic_update_slice_in_dim(
                    zero_cols, grad_kernel[:, :local_inner], col_start, 1
                ),
                grad_kernel[:, local_inner:],
            ],
            axis=1,
        )
        zero_bias = jnp.zeros((INNER,), jnp.float32)
        grad_conv_b = jnp.concatenate(
            [
                lax.dynamic_update_slice_in_dim(zero_bias, grad_offset[:local_inner], col_start, 0),
                grad_offset[local_inner:],
            ]
        )
        head_parts[layer_idx] = lax.psum((grad_shift, grad_rate, grad_skip), "batch")
        weight_parts[layer_idx] = (
            grad_ngain,
            grad_in,
            grad_conv_w,
            grad_conv_b,
            grad_ggain,
            grad_out,
        )
    stacked = tuple((jnp.stack([weight_parts[i][k] for i in range(layers)]) for k in range(6)))
    partial_sums = (
        lax.psum_scatter(
            stacked[0].astype(jnp.bfloat16), "batch", scatter_dimension=1, tiled=True
        ).astype(jnp.float32),
        lax.psum_scatter(
            stacked[1].astype(jnp.bfloat16), "batch", scatter_dimension=1, tiled=True
        ).astype(jnp.float32),
        lax.psum_scatter(
            stacked[2].astype(jnp.bfloat16), "batch", scatter_dimension=2, tiled=True
        ).astype(jnp.float32),
        lax.psum_scatter(
            stacked[3].astype(jnp.bfloat16), "batch", scatter_dimension=1, tiled=True
        ).astype(jnp.float32),
        lax.psum_scatter(
            stacked[4].astype(jnp.bfloat16), "batch", scatter_dimension=1, tiled=True
        ).astype(jnp.float32),
        lax.psum_scatter(
            stacked[5].astype(jnp.bfloat16), "batch", scatter_dimension=1, tiled=True
        ).astype(jnp.float32),
    )
    stacked = (
        lax.psum_scatter(
            partial_sums[0].astype(jnp.bfloat16), "seq", scatter_dimension=1, tiled=True
        ).astype(jnp.float32),
        lax.psum_scatter(
            partial_sums[1].astype(jnp.bfloat16), "seq", scatter_dimension=1, tiled=True
        ).astype(jnp.float32),
        lax.psum_scatter(
            partial_sums[2].astype(jnp.bfloat16), "seq", scatter_dimension=2, tiled=True
        ).astype(jnp.float32),
        lax.psum_scatter(
            partial_sums[3].astype(jnp.bfloat16), "seq", scatter_dimension=1, tiled=True
        ).astype(jnp.float32),
        lax.psum_scatter(
            partial_sums[4].astype(jnp.bfloat16), "seq", scatter_dimension=1, tiled=True
        ).astype(jnp.float32),
        lax.psum_scatter(
            partial_sums[5].astype(jnp.bfloat16), "seq", scatter_dimension=1, tiled=True
        ).astype(jnp.float32),
    )
    heads_stacked = tuple((jnp.stack([head_parts[i][k] for i in range(layers)]) for k in range(3)))
    return (
        stream,
        upstream,
        stacked[0],
        stacked[1],
        stacked[2],
        stacked[3],
        heads_stacked[0],
        heads_stacked[1],
        heads_stacked[2],
        stacked[4],
        stacked[5],
    )


def solution(mesh):
    in_specs = (
        P(("batch", "seq"), None),
        P(("batch", "seq"), None),
        P(None, ("batch", "seq")),
        P(None, ("batch", "seq"), None),
        P(None, None, ("batch", "seq")),
        P(None, ("batch", "seq")),
        P(None, "seq"),
        P(None, "seq"),
        P(None, "seq"),
        P(None, ("batch", "seq")),
        P(None, ("batch", "seq"), None),
    )
    out_specs = (
        P(("batch", "seq"), None),
        P(("batch", "seq"), None),
        P(None, ("batch", "seq")),
        P(None, ("batch", "seq"), None),
        P(None, None, ("batch", "seq")),
        P(None, ("batch", "seq")),
        P(None, "seq"),
        P(None, "seq"),
        P(None, "seq"),
        P(None, ("batch", "seq")),
        P(None, ("batch", "seq"), None),
    )
    return jax.shard_map(local, mesh=mesh, in_specs=in_specs, out_specs=out_specs, check_vma=False)
```

profile of v0, /device:TPU:0, one launch (start us, length us, event | category | flops | bytes accessed | tf_op | source)
XLA Modules:
  0.0 1634.4 jit_solution(17287218793255971408)
XLA Ops:
  12.8 43.6 %all-reduce.36 = (bf16[1024]{0:T(1024)(128)(2,1)S(1)}, bf16[2304]{0:T(1024)(128)(2,1)S(1)}, bf16[2048]{0:T(1024)(128)(2,1)}, bf16[1024]{0:T(1024)(128)(2,1)}, bf...) all-reduce(bf16[1024]{0:T(1024)(128)(2,1)S(1)} %dynamic-update-slic, ...), channel_id=4, replica_groups=mesh['batch'=4,'seq'=8] {'batch','seq'}, use_global_device_ids=true, to_apply=%add.27 | all-reduce | flops 10752 | bytes 43008
  57.1 37.6 %all-gather.23.cloned.1.call-done = bf16[1,1024,4384]{2,1,0:T(8,128)(2,1)} async-done(((bf16[1,32,4384]{2,1,0:T(8,128)(2,1)}), bf16[1,1024,4384]{2,1,0:T(8,128)(2,1)}) %all-gather.23.cloned.1.call-update) | async-done | bytes 8978448 | tf_op jit(solution)/shard_map/all_gather | solution.py:112
  94.7 7.4 fusion.46
  105.8 47.1 %all-gather.1 = bf16[1,4,2304]{1,0,2:T(2,128)(2,1)S(1)} all-gather(bf16[1,4,72]{1,0,2:T(2,128)(2,1)S(1)} %copy.1540), channel_id=3, replica_groups=mesh['batch'=4,'seq'=8] {'batch','seq'}, dimensions={2}, use_global_device_ids=true | all-gather | bytes 19008 | tf_op jit(solution)/shard_map/all_gather | solution.py:113
  154.3 48.1 %all-gather.7 = bf16[1,4,2304]{1,0,2:T(2,128)(2,1)S(1)} all-gather(bf16[1,4,72]{1,0,2:T(2,128)(2,1)S(1)} %copy.1539), channel_id=9, replica_groups=mesh['batch'=4,'seq'=8] {'batch','seq'}, dimensions={2}, use_global_device_ids=true | all-gather | bytes 19008 | tf_op jit(solution)/shard_map/all_gather | solution.py:113
  230.5 28.3 %all-to-all-done = bf16[256,8,256]{0,2,1:T(8,128)(2,1)S(1)} async-done(((bf16[256,8,256]{0,2,1:T(8,128)(2,1)}), bf16[256,8,256]{0,2,1:T(8,128)(2,1)S(1)}, u32[]{:S(2)}, u32[]{:S(2)}) %all-to-all-start) | async-done | bytes 1048608 | tf_op jit(solution)/shard_map/all_to_all | solution.py:126
  266.6 5.7 multiply_convert_fusion.1
  277.8 6.4 while.94
  291.1 6.6 bitcast_add_fusion.11
  300.8 9.6 all-to-all-done.2
  326.1 26.4 %all-to-all-done.3 = bf16[8,256,256]{1,2,0:T(8,128)(2,1)S(1)} async-done(((bf16[8,256,256]{1,2,0:T(8,128)(2,1)}), bf16[8,256,256]{1,2,0:T(8,128)(2,1)S(1)}, u32[]{:S(2)}, u32[]{:S(2)}) %all-to-all-start.3) | async-done | bytes 1048608 | tf_op jit(solution)/shard_map/all_to_all | solution.py:156
  360.7 7.7 fusion.49
  400.9 15.1 all-to-all-done.4
  425.6 5.6 multiply_convert_fusion
  441.2 18.9 %while.95 = (s32[]{:T(128)}, f32[1,4,64,128]{3,2,1,0:T(8,128)S(1)}, f32[8,1,4,64,128]{4,3,2,1,0:T(8,128)}, f32[8,1,4]{2,1,0:T(1,128)}, f32[8,1,4,64,128]{4,3,2,1,0:T(8,128)}, /*index=5*/s32[]{:T(128)}, s32[]{:T(128)}) while((s32[]{:T(128)}, f32[1,4,64,128]{3,2,1,0:T(8,128)S(1)}, f32[8,1,4,64,128]{4,3,2,1,0:T(8,128)}, ...), condition=%wide.region_10.11_spmd.clone, body=%wide.region_9.10_spmd.clone.sunk | while | flops 131075 | bytes 655516 | solution.py:57
  469.2 6.6 bitcast_add_fusion.10
  494.3 5.0 all-to-all-start.7
  514.7 11.3 all-to-all-done.7
  533.0 4.8 multiply_reduce_fusion.12
  545.3 18.3 %while.96 = (s32[]{:T(128)}, f32[1,4,64,128]{3,2,1,0:T(8,128)S(1)}, f32[8,1,4,64,128]{4,3,2,1,0:T(8,128)S(1)}, f32[8,1,4,1,1]{2,4,3,1,0:T(1,128)S(1)}, f32[8,1,4...) while((s32[]{:T(128)}, f32[1,4,64,128]{3,2,1,0:T(8,128)S(1)}, ...), condition=%wide.region_15.17_spmd.clone, body=%wide.region_14.16_spmd.clone.sunk | while | flops 131075 | bytes 656056 | solution.py:57
  563.6 8.1 all-to-all-done.8
  579.6 13.8 fusion.53
  599.8 14.4 while.97
  624.9 10.3 reduce-window.50
  635.4 6.3 fusion.171
  671.2 8.4 bitcast_add_fusion.9
  682.4 10.4 bitcast_add_fusion.8
  703.9 6.2 multiply_reduce_fusion.6
  712.7 7.0 fusion.114
  723.5 5.0 all-to-all-start.10
  730.8 31.5 %all-to-all-done.10 = bf16[8,256,256]{1,2,0:T(8,128)(2,1)S(1)} async-done(((bf16[8,256,256]{1,2,0:T(8,128)(2,1)}), bf16[8,256,256]{1,2,0:T(8,128)(2,1)S(1)}, u32[]{:S(2)}, u32[]{:S(2)}) %all-to-all-start.10) | async-done | bytes 1048608 | tf_op jit(solution)/shard_map/all_to_all | solution.py:196
  784.1 9.0 all-to-all-done.9
  793.2 8.0 multiply_reduce_fusion.22
  808.8 4.7 all-to-all-start.12
  815.3 32.0 %while.98 = (s32[]{:T(128)}, f32[1,4,64,128]{3,2,1,0:T(8,128)S(1)}, f32[8,1,4,64,128]{4,3,2,1,0:T(8,128)}, f32[8,1,4,1,1]{2,4,3,1,0:T(1,128)}, f32[8,1,4]{2,1,0:...) while((s32[]{:T(128)}, f32[1,4,64,128]{3,2,1,0:T(8,128)S(1)}, ...), condition=%wide.region_34.36_spmd.clone, body=%wide.region_33.35_spmd.clone.sunk | while | flops 131075 | bytes 918696 | solution.py:57
  855.0 13.4 fusion.55
  875.3 19.3 %while.99 = (s32[]{:T(128)}, f32[1,4,64,128]{3,2,1,0:T(8,128)S(1)}, f32[8,1,4,64,128]{4,3,2,1,0:T(8,128)}, f32[8,1,4]{2,1,0:T(1,128)S(1)}, f32[8,1,4,64,128]{4,3...) while((s32[]{:T(128)}, f32[1,4,64,128]{3,2,1,0:T(8,128)S(1)}, ...), condition=%wide.region_38.40_spmd.clone, body=%wide.region_36.39_spmd.clone.sunk | while | flops 196608 | bytes 1049812 | solution.py:57
  905.3 10.1 reduce-window.56
  915.5 6.4 fusion.177
  928.7 5.1 all-to-all-start.15
  952.1 8.4 bitcast_add_fusion.7
  963.2 10.6 bitcast_add_fusion.6
  985.0 5.6 multiply_reduce_fusion.10
  993.4 7.0 fusion.115
  1004.3 5.3 all-to-all-start.14
  1011.9 31.9 %all-to-all-done.14 = bf16[8,256,256]{1,2,0:T(8,128)(2,1)} async-done(((bf16[8,256,256]{1,2,0:T(8,128)(2,1)}), bf16[8,256,256]{1,2,0:T(8,128)(2,1)}, u32[]{:S(2)}, u32[]{:S(2)}) %all-to-all-start.14) | async-done | bytes 1048608 | tf_op jit(solution)/shard_map/all_to_all | solution.py:196
  1048.2 4.8 convert_bitcast_fusion
  1054.2 4.9 convert_bitcast_fusion.1
  1059.1 15.5 all-to-all-done.13
  1074.6 8.3 multiply_reduce_fusion.23
  1083.9 7.5 pad_maximum_fusion.1
  1096.9 7.7 fusion.44
  1104.7 11.5 pad_maximum_fusion
  1125.2 71.6 %reduce-scatter.32.cloned.1.call-done = bf16[2,512,1024]{2,1,0:T(8,128)(2,1)} async-done(((bf16[2,2048,1024]{2,1,0:T(8,128)(2,1)}), bf16[2,512,1024]{2,1,0:T(8,128)(2,1)}) %reduce-scatter.32.cloned.1.call-update) | async-done | bytes 2097168 | tf_op jit(solution)/shard_map/reduce_scatter | solution.py:270
  1196.9 166.3 %reduce-scatter.30.cloned.1.call-done = bf16[2,256,4384]{1,2,0:T(8,128)(2,1)} async-done(((bf16[2,1024,4384]{1,2,0:T(8,128)(2,1)}), bf16[2,256,4384]{1,2,0:T(8,128)(2,1)}) %reduce-scatter.30.cloned.1.call-update) | async-done | bytes 4489232 | tf_op jit(solution)/shard_map/reduce_scatter | solution.py:258
  1363.2 12.5 copy.1465
  1378.2 4.8 fusion.189
  1383.2 12.8 reduce-scatter.46.cloned.1.call-done
  1397.6 9.8 all-reduce.35
  1409.2 13.1 reduce-scatter.42.cloned.1.call-done
  1423.3 27.7 %reduce-scatter.40.cloned.1.call-done = bf16[576,8]{1,0:T(8,128)(2,1)} async-done(((bf16[2304,8]{1,0:T(8,128)(2,1)}), bf16[576,8]{1,0:T(8,128)(2,1)}) %reduce-scatter.40.cloned.1.call-update) | async-done | bytes 9232
  1452.3 28.2 %all-reduce.37 = (bf16[2,4,576]{2,1,0:T(4,128)(2,1)S(1)}, bf16[2,576]{1,0:T(2,128)(2,1)S(1)}) all-reduce(bf16[2,4,576]{2,1,0:T(4,128)(2,1)S(1)} %copy.1526, bf16[2,576]{1,0:T(2,128)(2,1)S(1)} %copy.1530), channel_id=21, replica_groups=mesh['batch'=4,'seq'=8] {'seq'}, use_global_device_ids=true, to_apply=%region_65.67.clone | all-reduce | flops 5760 | bytes 23040
  1486.0 33.8 %reduce-scatter.34.cloned.1.call-done = bf16[2,64,1024]{2,1,0:T(8,128)(2,1)} async-done(((bf16[2,512,1024]{2,1,0:T(8,128)(2,1)}), bf16[2,64,1024]{2,1,0:T(8,128)(2,1)}) %reduce-scatter.34.cloned.1.call-update) | async-done | bytes 262160 | tf_op jit(solution)/shard_map/reduce_scatter | solution.py:290
  1521.5 103.2 %all-reduce.40.cloned.1.call-done = bf16[2,256,4384]{2,0,1:T(2,128)(2,1)} async-done(((bf16[2,256,4384]{2,0,1:T(2,128)(2,1)}), bf16[2,256,4384]{2,0,1:T(2,128)(2,1)}) %all-reduce.40.cloned.1.call-update) | async-done | bytes 4489232
  (1005 shorter events, 521.5 us)
Async XLA Ops:
  7.2 49.2 %copy-start.31 = (f32[256,1024]{1,0:T(8,128)S(1)}, f32[256,1024]{1,0:T(8,128)}, u32[]{:S(2)}) copy-start(f32[256,1024]{1,0:T(8,128)} %param.24) | copy-start | bytes 3145732
  7.2 87.5 %all-gather.23.cloned.1.call-start = ((), (), s32[]{:S(2)}) async-start(), calls=%async_computation.34 | async-start | bytes 9461760 | tf_op jit(solution)/shard_map/all_gather | solution.py:112
  9.2 255.2 %all-gather.19.cloned.1.call-start = ((), (), s32[]{:S(2)}) async-start(), calls=%async_computation.27 | async-start | bytes 1179648 | tf_op jit(solution)/shard_map/all_gather | solution.py:130
  56.4 45.7 %copy-start.124 = (f32[1024]{0:T(1024)}, f32[1024]{0:T(1024)S(1)}, u32[]{:S(2)}) copy-start(f32[1024]{0:T(1024)S(1)} %convert_element_type.624) | copy-start | bytes 12292
  57.1 45.0 %copy-start.159 = (f32[256]{0:T(256)}, f32[256]{0:T(256)S(1)}, u32[]{:S(2)}) copy-start(f32[256]{0:T(256)S(1)} %fusion.274) | copy-start | bytes 3076
  57.1 47.1 %copy-start.85 = (bf16[2,64,1024]{2,1,0:T(8,128)(2,1)S(1)}, bf16[2,64,1024]{2,1,0:T(8,128)(2,1)}, u32[]{:S(2)}) copy-start(bf16[2,64,1024]{2,1,0:T(8,128)(2,1)} %param.34) | copy-start | bytes 786436
  57.1 48.5 %copy-start.172 = (bf16[2,4,72]{2,1,0:T(4,128)(2,1)S(1)}, bf16[2,4,72]{2,1,0:T(4,128)(2,1)}, u32[]{:S(2)}) copy-start(bf16[2,4,72]{2,1,0:T(4,128)(2,1)} %param.28) | copy-start | bytes 3460
  104.2 252.1 %all-gather.25.cloned.1.call-start = ((), (), s32[]{:S(2)}) async-start(), calls=%async_computation.35 | async-start | bytes 4325376 | tf_op jit(solution)/shard_map/all_gather | solution.py:116
  105.0 255.7 %all-gather.27.cloned.1.call-start = ((), (), s32[]{:S(2)}) async-start(), calls=%async_computation.36 | async-start | bytes 9461760 | tf_op jit(solution)/shard_map/all_gather | solution.py:112
  105.7 98.1 %copy-start.175 = (f32[2,4]{1,0:T(2,128)S(1)}, f32[2,4]{1,0:T(2,128)}, u32[]{:S(2)}) copy-start(f32[2,4]{1,0:T(2,128)} %param.32) | copy-start | bytes 100
  105.7 100.1 %copy-start.176 = (f32[2,4]{1,0:T(2,128)S(1)}, f32[2,4]{1,0:T(2,128)}, u32[]{:S(2)}) copy-start(f32[2,4]{1,0:T(2,128)} %param.30) | copy-start | bytes 100
  105.7 100.6 %copy-start.166 = (f32[2,4]{1,0:T(2,128)S(1)}, f32[2,4]{1,0:T(2,128)}, u32[]{:S(2)}) copy-start(f32[2,4]{1,0:T(2,128)} %param.31) | copy-start | bytes 100
  105.7 101.2 %slice-start = ((bf16[256,4384]{0,1:T(8,128)(2,1)}), bf16[256,32]{0,1:T(8,128)(2,1)S(1)}, s32[]{:S(2)}) async-start(bf16[256,4384]{0,1:T(8,128)(2,1)} %copy-done.63), calls=%async_computation.45 | async-start | bytes 32768 | tf_op jit(solution)/shard_map/slice | solution.py:124
  206.9 59.7 %copy-start.110 = (f32[1,512]{1,0:T(1,128)}, f32[1,512]{1,0:T(1,128)S(1)}, u32[]{:S(2)}) copy-start(f32[1,512]{1,0:T(1,128)S(1)} %get-tuple-element.1233) | copy-start | bytes 6148
  206.9 59.7 %copy-start.112 = (f32[1,512]{1,0:T(1,128)}, f32[1,512]{1,0:T(1,128)S(1)}, u32[]{:S(2)}) copy-start(f32[1,512]{1,0:T(1,128)S(1)} %get-tuple-element.1234) | copy-start | bytes 6148
  206.9 59.7 %copy-start.114 = (f32[1,512]{1,0:T(1,128)}, f32[1,512]{1,0:T(1,128)S(1)}, u32[]{:S(2)}) copy-start(f32[1,512]{1,0:T(1,128)S(1)} %get-tuple-element.1235) | copy-start | bytes 6148
  206.9 59.7 %copy-start.116 = (f32[1,512]{1,0:T(1,128)}, f32[1,512]{1,0:T(1,128)S(1)}, u32[]{:S(2)}) copy-start(f32[1,512]{1,0:T(1,128)S(1)} %get-tuple-element.1236) | copy-start | bytes 6148
  207.5 9.0 all-to-all-start.1
  216.5 42.3 %all-to-all-start = ((bf16[256,8,256]{0,2,1:T(8,128)(2,1)}), bf16[256,8,256]{0,2,1:T(8,128)(2,1)S(1)}, u32[]{:S(2)}, u32[]{:S(2)}) async-start(bf16[256,8,256]{0,2,1:T(8,128)(2,1)} %bitcast.6), calls=%async_computation | async-start | bytes 2097152 | tf_op jit(solution)/shard_map/all_to_all | solution.py:126
  258.8 51.6 %all-to-all-start.2 = ((bf16[256,8,256]{0,2,1:T(8,128)(2,1)}), bf16[256,8,256]{0,2,1:T(8,128)(2,1)}, u32[]{:S(2)}, u32[]{:S(2)}) async-start(bf16[256,8,256]{0,2,1:T(8,128)(2,1)} %bitcast.39), calls=%async_computation.2 | async-start | bytes 2097152 | tf_op jit(solution)/shard_map/all_to_all | solution.py:127
  322.4 30.1 %all-to-all-start.3 = ((bf16[8,256,256]{1,2,0:T(8,128)(2,1)}), bf16[8,256,256]{1,2,0:T(8,128)(2,1)S(1)}, u32[]{:S(2)}, u32[]{:S(2)}) async-start(bf16[8,256,256]{1,2,0:T(8,128)(2,1)} %copy.1331), calls=%async_computation.3 | async-start | bytes 2097152 | tf_op jit(solution)/shard_map/all_to_all | solution.py:156
  326.0 97.5 %all-gather.21.cloned.1.call-start = ((), (), s32[]{:S(2)}) async-start(), calls=%async_computation.28 | async-start | bytes 1179648 | tf_op jit(solution)/shard_map/all_gather | solution.py:130
  326.1 34.6 %copy-start.126 = (f32[1024]{0:T(1024)}, f32[1024]{0:T(1024)S(1)}, u32[]{:S(2)}) copy-start(f32[1024]{0:T(1024)S(1)} %convert_element_type.626) | copy-start | bytes 12292
  370.5 162.5 %all-gather.29.cloned.1.call-start = ((), (), s32[]{:S(2)}) async-start(), calls=%async_computation.37 | async-start | bytes 4325376 | tf_op jit(solution)/shard_map/all_gather | solution.py:116
  372.6 53.0 %copy-start.118 = (f32[1,512]{1,0:T(1,128)}, f32[1,512]{1,0:T(1,128)S(1)}, u32[]{:S(2)}) copy-start(f32[1,512]{1,0:T(1,128)S(1)} %get-tuple-element.1231) | copy-start | bytes 6148
  372.6 53.0 %copy-start.120 = (f32[1,512]{1,0:T(1,128)}, f32[1,512]{1,0:T(1,128)S(1)}, u32[]{:S(2)}) copy-start(f32[1,512]{1,0:T(1,128)S(1)} %get-tuple-element.1232) | copy-start | bytes 6148
  373.3 164.4 %copy-start.76 = (f32[2048]{0:T(1024)}, f32[2048]{0:T(1024)S(1)}, u32[]{:S(2)}) copy-start(f32[2048]{0:T(1024)S(1)} %convert_element_type.627) | copy-start | bytes 24580
  374.7 9.1 all-to-all-start.5
  383.8 32.3 %all-to-all-start.4 = ((bf16[256,8,256]{0,2,1:T(8,128)(2,1)}), bf16[256,8,256]{0,2,1:T(8,128)(2,1)S(1)}, u32[]{:S(2)}, u32[]{:S(2)}) async-start(bf16[256,8,256]{0,2,1:T(8,128)(2,1)} %bitcast.996), calls=%async_computation.4 | async-start | bytes 2097152 | tf_op jit(solution)/shard_map/all_to_all | solution.py:126
  400.9 98.3 %copy-start.81 = (f32[256,8,4]{0,2,1:T(4,128)}, f32[256,8,4]{0,2,1:T(4,128)S(1)}, u32[]{:S(2)}) copy-start(f32[256,8,4]{0,2,1:T(4,128)S(1)} %convert_element_type.529) | copy-start | bytes 98308
  416.1 65.3 %all-to-all-start.6 = ((bf16[256,8,256]{0,2,1:T(8,128)(2,1)}), bf16[256,8,256]{0,2,1:T(8,128)(2,1)}, u32[]{:S(2)}, u32[]{:S(2)}) async-start(bf16[256,8,256]{0,2,1:T(8,128)(2,1)} %bitcast.995), calls=%async_computation.6 | async-start | bytes 2097152 | tf_op jit(solution)/shard_map/all_to_all | solution.py:127
  437.6 73.5 %copy-start.6 = (f32[32,8,8,256]{3,2,1,0:T(8,128)}, f32[32,8,8,256]{3,2,1,0:T(8,128)S(1)}, u32[]{:S(2)}) copy-start(f32[32,8,8,256]{3,2,1,0:T(8,128)S(1)} %copy.1557) | copy-start | bytes 6291460
  494.3 31.7 %all-to-all-start.7 = ((bf16[8,256,256]{1,2,0:T(8,128)(2,1)}), bf16[8,256,256]{1,2,0:T(8,128)(2,1)}, u32[]{:S(2)}, u32[]{:S(2)}) async-start(bf16[8,256,256]{1,2,0:T(8,128)(2,1)} %copy.1359), calls=%async_computation.7 | async-start | bytes 2097152 | tf_op jit(solution)/shard_map/all_to_all | solution.py:156
  541.5 30.2 %all-to-all-start.8 = ((bf16[256,8,256]{0,2,1:T(8,128)(2,1)}), bf16[256,8,256]{0,2,1:T(8,128)(2,1)S(1)}, u32[]{:S(2)}, u32[]{:S(2)}) async-start(bf16[256,8,256]{0,2,1:T(8,128)(2,1)} %bitcast.115), calls=%async_computation.8 | async-start | bytes 2097152 | tf_op jit(solution)/shard_map/all_to_all | solution.py:183
  649.6 73.9 %all-to-all-start.11 = ((bf16[8,256,4]{1,2,0:T(4,128)(2,1)}), bf16[8,256,4]{1,2,0:T(4,128)(2,1)S(1)}, u32[]{:S(2)}, u32[]{:S(2)}) async-start(bf16[8,256,4]{1,2,0:T(4,128)(2,1)} %bitcast.163), calls=%async_computation.12 | async-start | bytes 32768 | tf_op jit(solution)/shard_map/all_to_all | solution.py:210
  723.5 38.8 %all-to-all-start.10 = ((bf16[8,256,256]{1,2,0:T(8,128)(2,1)}), bf16[8,256,256]{1,2,0:T(8,128)(2,1)S(1)}, u32[]{:S(2)}, u32[]{:S(2)}) async-start(bf16[8,256,256]{1,2,0:T(8,128)(2,1)} %bitcast.912), calls=%async_computation.10 | async-start | bytes 2097152 | tf_op jit(solution)/shard_map/all_to_all | solution.py:196
  728.5 64.6 %reduce-scatter.26.cloned.1.call-start = ((), (), s32[]{:S(2)}) async-start(), calls=%async_computation.29 | async-start | bytes 1179648 | tf_op jit(solution)/shard_map/reduce_scatter | solution.py:218
  728.8 37.7 %copy-start.83 = (f32[256,8,4]{0,2,1:T(4,128)}, f32[256,8,4]{0,2,1:T(4,128)S(1)}, u32[]{:S(2)}) copy-start(f32[256,8,4]{0,2,1:T(4,128)S(1)} %convert_element_type.509) | copy-start | bytes 98308
  729.6 37.0 %copy-start.153 = (f32[4]{0:T(128)S(1)}, f32[4]{0:T(128)}, u32[]{:S(2)}) copy-start(f32[4]{0:T(128)} %copy-done.152) | copy-start | bytes 52
  729.6 37.4 %copy-start.142 = (f32[4]{0:T(128)S(1)}, f32[4]{0:T(128)}, u32[]{:S(2)}) copy-start(f32[4]{0:T(128)} %copy-done.141) | copy-start | bytes 52
  762.3 30.8 %all-to-all-start.9 = ((bf16[8,256,256]{1,2,0:T(8,128)(2,1)}), bf16[8,256,256]{1,2,0:T(8,128)(2,1)}, u32[]{:S(2)}, u32[]{:S(2)}) async-start(bf16[8,256,256]{1,2,0:T(8,128)(2,1)} %copy.1384), calls=%async_computation.9 | async-start | bytes 2097152 | tf_op jit(solution)/shard_map/all_to_all | solution.py:203
  808.8 38.4 %all-to-all-start.12 = ((bf16[256,8,256]{0,2,1:T(8,128)(2,1)}), bf16[256,8,256]{0,2,1:T(8,128)(2,1)}, u32[]{:S(2)}, u32[]{:S(2)}) async-start(bf16[256,8,256]{0,2,1:T(8,128)(2,1)} %bitcast.990), calls=%async_computation.13 | async-start | bytes 2097152 | tf_op jit(solution)/shard_map/all_to_all | solution.py:183
  928.7 75.6 %all-to-all-start.15 = ((bf16[8,256,4]{1,2,0:T(4,128)(2,1)}), bf16[8,256,4]{1,2,0:T(4,128)(2,1)S(1)}, u32[]{:S(2)}, u32[]{:S(2)}) async-start(bf16[8,256,4]{1,2,0:T(4,128)(2,1)} %bitcast.238), calls=%async_computation.17 | async-start | bytes 32768 | tf_op jit(solution)/shard_map/all_to_all | solution.py:210
  1004.3 39.5 %all-to-all-start.14 = ((bf16[8,256,256]{1,2,0:T(8,128)(2,1)}), bf16[8,256,256]{1,2,0:T(8,128)(2,1)}, u32[]{:S(2)}, u32[]{:S(2)}) async-start(bf16[8,256,256]{1,2,0:T(8,128)(2,1)} %bitcast.911), calls=%async_computation.15 | async-start | bytes 2097152 | tf_op jit(solution)/shard_map/all_to_all | solution.py:196
  1009.6 65.0 %reduce-scatter.28.cloned.1.call-start = ((), (), s32[]{:S(2)}) async-start(), calls=%async_computation.30 | async-start | bytes 1179648 | tf_op jit(solution)/shard_map/reduce_scatter | solution.py:218
  1010.7 37.4 %copy-start.122 = (bf16[2048]{0:T(1024)(128)(2,1)S(1)}, bf16[2048]{0:T(1024)(128)(2,1)}, u32[]{:S(2)}) copy-start(bf16[2048]{0:T(1024)(128)(2,1)} %get-tuple-element.1045) | copy-start | bytes 12292
  1010.7 37.4 %copy-start.1 = (f32[256,2048]{1,0:T(8,128)S(1)}, f32[256,2048]{1,0:T(8,128)}, u32[]{:S(2)}) copy-start(f32[256,2048]{1,0:T(8,128)} %copy-done) | copy-start | bytes 6291460
  1010.7 37.4 %copy-start.77 = (f32[2048]{0:T(1024)S(1)}, f32[2048]{0:T(1024)}, u32[]{:S(2)}) copy-start(f32[2048]{0:T(1024)} %copy-done.76) | copy-start | bytes 24580
  1010.7 37.4 %copy-start.89 = (f32[256]{0:T(256)S(1)}, f32[256]{0:T(256)}, u32[]{:S(2)}) copy-start(f32[256]{0:T(256)} %copy-done.88) | copy-start | bytes 3076
  1043.8 30.8 %all-to-all-start.13 = ((bf16[8,256,256]{1,2,0:T(8,128)(2,1)}), bf16[8,256,256]{1,2,0:T(8,128)(2,1)}, u32[]{:S(2)}, u32[]{:S(2)}) async-start(bf16[8,256,256]{1,2,0:T(8,128)(2,1)} %copy.1436), calls=%async_computation.14 | async-start | bytes 2097152 | tf_op jit(solution)/shard_map/all_to_all | solution.py:203
  1048.0 69.2 %reduce-scatter.44.cloned.1.call-start = ((), (), s32[]{:S(2)}) async-start(), calls=%async_computation.42 | async-start | bytes 655360
  1054.1 20.5 %copy-start.125 = (f32[1024]{0:T(1024)S(1)}, f32[1024]{0:T(1024)}, u32[]{:S(2)}) copy-start(f32[1024]{0:T(1024)} %copy-done.124) | copy-start | bytes 12292
  1054.1 20.5 %copy-start.160 = (f32[256]{0:T(256)S(1)}, f32[256]{0:T(256)}, u32[]{:S(2)}) copy-start(f32[256]{0:T(256)} %copy-done.159) | copy-start | bytes 3076
  1054.1 70.6 %reduce-scatter.36.cloned.1.call-start = ((), (), s32[]{:S(2)}) async-start(), calls=%async_computation.38 | async-start | bytes 327680
  1083.8 113.0 %reduce-scatter.32.cloned.1.call-start = ((), (), s32[]{:S(2)}) async-start(), calls=%async_computation.32 | async-start | bytes 10485760 | tf_op jit(solution)/shard_map/reduce_scatter | solution.py:270
  1091.4 271.7 %reduce-scatter.30.cloned.1.call-start = ((), (), s32[]{:S(2)}) async-start(), calls=%async_computation.31 | async-start | bytes 22446080 | tf_op jit(solution)/shard_map/reduce_scatter | solution.py:258
  1116.2 279.8 %reduce-scatter.46.cloned.1.call-start = ((), (), s32[]{:S(2)}) async-start(), calls=%async_computation.43 | async-start | bytes 147456
  1117.3 305.0 %reduce-scatter.42.cloned.1.call-start = ((), (), s32[]{:S(2)}) async-start(), calls=%async_computation.41 | async-start | bytes 737280
  1119.0 332.1 %reduce-scatter.40.cloned.1.call-start = ((), (), s32[]{:S(2)}) async-start(), calls=%async_computation.40 | async-start | bytes 737280
  1124.6 360.0 %reduce-scatter.38.cloned.1.call-start = ((), (), s32[]{:S(2)}) async-start(), calls=%async_computation.39 | async-start | bytes 73728
  1125.2 394.6 %reduce-scatter.34.cloned.1.call-start = ((), (), s32[]{:S(2)}) async-start(), calls=%async_computation.33 | async-start | bytes 2359296 | tf_op jit(solution)/shard_map/reduce_scatter | solution.py:290
  1196.8 427.9 %all-reduce.40.cloned.1.call-start = ((), (), s32[]{:S(2)}) async-start(), calls=%async_computation.44 | async-start | bytes 9175040
  1378.2 19.4 %copy-start.174 = (f32[4]{0:T(128)S(1)}, f32[4]{0:T(128)}, u32[]{:S(2)}) copy-start(f32[4]{0:T(128)} %get-tuple-element.1143) | copy-start | bytes 52
  1378.2 103.6 %copy-start.133 = (f32[256]{0:T(256)S(1)}, f32[256]{0:T(256)}, u32[]{:S(2)}) copy-start(f32[256]{0:T(256)} %copy-done.132) | copy-start | bytes 3076
  (151 other events, 759.1 us)
Sparse Core Ops, SparseCore 0:
  11.4 83.2 all-gather.22
  104.3 25.0 all-gather.18
  132.4 63.8 all-gather.24
  199.0 112.4 all-gather.26
  370.6 25.8 all-gather.20
  399.3 70.1 all-gather.28
  732.2 34.9 reduce-scatter.25
  1012.7 34.7 reduce-scatter.27
  1054.2 25.5 reduce-scatter.43
  1083.9 23.3 reduce-scatter.35
  1110.5 86.3 reduce-scatter.31
  1199.8 163.2 reduce-scatter.29
  1365.4 30.5 reduce-scatter.45
  1398.7 23.5 reduce-scatter.41
  1425.6 25.3 reduce-scatter.39
  1453.1 30.5 reduce-scatter.37
  1485.9 33.8 reduce-scatter.33
  1522.0 102.7 all-reduce.39
where the time goes:
time: 1650 us; the launch traced here: 1630 us
  waiting for transfers between devices  661 us (40%)
  local copies, waits for them, and re-layouts  249 us (15%)
  other arithmetic  245 us (15%)
  matrix products  215 us (13%)
  blocking collectives  177 us (11%)
  starting transfers between devices  68 us (4%)
  between operations  18.7 us (1%)
    reduce_scatter x1, waiting for transfers between devices, local(): lax.psum_scatter(stacked[1].astype(jnp.bfloat16), 'batch', scatter_dimens...  166 us
    unnamed x25, waiting for transfers between devices  160 us
    all_gather x2, blocking collectives, local(): lax.all_gather(conv_weight[layer_idx], ('batch', 'seq'), axis=1, tiled=True)  95.1 us
    dot_general x8, matrix products, state_space(): within = jnp.einsum('chts,cshp->cthp', mixing, blocked, precision=HIGHEST)  78.2 us
    unnamed x2, blocking collectives  71.8 us
    reduce_scatter x1, waiting for transfers between devices, local(): lax.psum_scatter(stacked[5].astype(jnp.bfloat16), 'batch', scatter_dimens...  71.6 us
    all_to_all x2, waiting for transfers between devices, local(): lax.all_to_all(d_signal[:, :local_inner].astype(jnp.bfloat16), 'seq', spl...  63.3 us
    unnamed x413, local copies, waits for them, and re-layouts  52 us
  transfers between devices with their start and end apart: 34, of which 20 were waited for; matrix products, arithmetic and copies ran while one was open for 30% of the time, Pallas kernels for 0%

commit v1 on v0

--- a/solution.py
+++ b/solution.py
@@ -9,6 +9,20 @@
 INNER = 2048
 EPS = 1e-05
 HIGHEST = lax.Precision.HIGHEST
+
+
+def proceed_sheets(work_x):
+    w_next, current_block = (lax.axis_size(("batch", "seq")), lax.axis_index(("batch", "seq")))
+    left_arr, met_up = (work_x, 1)
+    while met_up < w_next:
+        r_now = lax.ppermute(
+            left_arr, ("batch", "seq"), perm=[(dd, dd ^ met_up) for dd in range(w_next)]
+        )
+        heard = jnp.concatenate([left_arr, r_now], axis=1)
+        inter = jnp.concatenate([r_now, left_arr], axis=1)
+        left_arr = jnp.where(current_block & met_up == 0, heard, inter)
+        met_up = 2 * met_up
+    return left_arr
 
 
 def row_norm(rows, gain):
@@ -110,7 +124,7 @@
         gathered = (
             lax.all_gather(norm_gain[layer_idx], ("batch", "seq"), axis=0, tiled=True),
             lax.all_gather(in_proj[layer_idx], ("batch", "seq"), axis=0, tiled=True),
-            lax.all_gather(conv_weight[layer_idx], ("batch", "seq"), axis=1, tiled=True),
+            proceed_sheets(conv_weight[layer_idx]),
             lax.all_gather(conv_bias[layer_idx], ("batch", "seq"), axis=0, tiled=True),
             lax.all_gather(gate_gain[layer_idx], ("batch", "seq"), axis=0, tiled=True),
             lax.all_gather(out_proj[layer_idx], ("batch", "seq"), axis=0, tiled=True),

time: 1650 us -> 1580 us (0.958)
  blocking collectives: 177 us -> 81.5 us
  waiting for transfers between devices: 661 us -> 694 us
    all_gather x2 -> x0, blocking collectives: 95.1 us -> none  [local(): lax.all_gather(conv_weight[layer_idx], ('batch', 'seq'), axis=1, tiled=True)]
    all_gather x2, waiting for transfers between devices: 37.6 us -> 62.7 us  [local(): lax.all_gather(in_proj[layer_idx], ('batch', 'seq'), axis=0, tiled=True)]
    unnamed x413 -> x387, local copies, waits for them, and re-layouts: 52 us -> 49.3 us
  transfers between devices with their start and end apart: 34 -> 44, of which waited for: 20 -> 30; matrix products, arithmetic and copies ran while one was open for 30% -> 30% of each run, Pallas kernels for 0% -> 0%
where the time goes in v1:
time: 1580 us; the launch traced here: 1570 us
  waiting for transfers between devices  694 us (44%)
  other arithmetic  244 us (15%)
  local copies, waits for them, and re-layouts  235 us (15%)
  matrix products  215 us (14%)
  blocking collectives  81.5 us (5%)
  starting transfers between devices  78.4 us (5%)
  between operations  18.7 us (1%)
    reduce_scatter x1, waiting for transfers between devices, local(): lax.psum_scatter(stacked[1].astype(jnp.bfloat16), 'batch', scatter_dimens...  166 us
    unnamed x25, waiting for transfers between devices  159 us
    dot_general x8, matrix products, state_space(): within = jnp.einsum('chts,cshp->cthp', mixing, blocked, precision=HIGHEST)  78.2 us
    reduce_scatter x1, waiting for transfers between devices, local(): lax.psum_scatter(stacked[5].astype(jnp.bfloat16), 'batch', scatter_dimens...  72.2 us
    unnamed x2, blocking collectives  71.6 us
    all_to_all x2, waiting for transfers between devices, local(): lax.all_to_all(d_signal[:, :local_inner].astype(jnp.bfloat16), 'seq', spl...  62.7 us
    all_gather x2, waiting for transfers between devices, local(): lax.all_gather(in_proj[layer_idx], ('batch', 'seq'), axis=0, tiled=True)  62.7 us
    unnamed x387, local copies, waits for them, and re-layouts  49.3 us
  transfers between devices with their start and end apart: 44, of which 30 were waited for; matrix products, arithmetic and copies ran while one was open for 30% of the time, Pallas kernels for 0%

profile of v1, /device:TPU:0, one launch (start us, length us, event | category | flops | bytes accessed | tf_op | source)
XLA Modules:
  0.0 1568.7 jit_solution(2902069534145710987)
XLA Ops:
  12.8 43.3 %all-reduce.36 = (bf16[1024]{0:T(1024)(128)(2,1)S(1)}, bf16[2304]{0:T(1024)(128)(2,1)S(1)}, bf16[2048]{0:T(1024)(128)(2,1)S(1)}, bf16[1024]{0:T(1024)(128)(2,1)S...) all-reduce(bf16[1024]{0:T(1024)(128)(2,1)S(1)} %dynamic-update-slic, ...), channel_id=3, replica_groups=mesh['batch'=4,'seq'=8] {'batch','seq'}, use_global_device_ids=true, to_apply=%add.27 | all-reduce | flops 10752 | bytes 43008
  57.0 37.7 %all-gather.21.cloned.1.call-done = bf16[1,1024,4384]{2,1,0:T(8,128)(2,1)} async-done(((bf16[1,32,4384]{2,1,0:T(8,128)(2,1)}), bf16[1,1024,4384]{2,1,0:T(8,128)(2,1)}) %all-gather.21.cloned.1.call-update) | async-done | bytes 8978448 | tf_op jit(solution)/shard_map/all_gather | solution.py:126
  94.7 7.4 fusion.46
  145.4 26.9 %all-to-all-done = bf16[256,8,256]{0,2,1:T(8,128)(2,1)S(1)} async-done(((bf16[256,8,256]{0,2,1:T(8,128)(2,1)}), bf16[256,8,256]{0,2,1:T(8,128)(2,1)S(1)}, u32[]{:S(2)}, u32[]{:S(2)}) %all-to-all-start) | async-done | bytes 1048608 | tf_op jit(solution)/shard_map/all_to_all | solution.py:140
  172.3 4.4 all-to-all-start.2
  180.1 5.7 multiply_convert_fusion.1
  199.5 6.6 bitcast_add_fusion.11
  229.1 38.7 %all-to-all-done.3 = bf16[8,256,256]{1,2,0:T(8,128)(2,1)S(1)} async-done(((bf16[8,256,256]{1,2,0:T(8,128)(2,1)}), bf16[8,256,256]{1,2,0:T(8,128)(2,1)S(1)}, u32[]{:S(2)}, u32[]{:S(2)}) %all-to-all-start.3) | async-done | bytes 1048608 | tf_op jit(solution)/shard_map/all_to_all | solution.py:170
  276.5 25.0 %all-gather.25.cloned.1.call-done = bf16[1,1024,4384]{2,1,0:T(8,128)(2,1)} async-done(((bf16[1,32,4384]{2,1,0:T(8,128)(2,1)}), bf16[1,1024,4384]{2,1,0:T(8,128)(2,1)}) %all-gather.25.cloned.1.call-update) | async-done | bytes 8978448 | tf_op jit(solution)/shard_map/all_gather | solution.py:126
  301.5 7.4 fusion.49
  339.2 15.2 all-to-all-done.4
  362.1 5.7 multiply_convert_fusion
  377.7 18.9 %while.95 = (s32[]{:T(128)}, f32[1,4,64,128]{3,2,1,0:T(8,128)S(1)}, f32[8,1,4,64,128]{4,3,2,1,0:T(8,128)}, f32[8,1,4]{2,1,0:T(1,128)}, f32[8,1,4,64,128]{4,3,2,1,0:T(8,128)}, /*index=5*/s32[]{:T(128)}, s32[]{:T(128)}) while((s32[]{:T(128)}, f32[1,4,64,128]{3,2,1,0:T(8,128)S(1)}, f32[8,1,4,64,128]{4,3,2,1,0:T(8,128)}, ...), condition=%wide.region_10.11_spmd.clone, body=%wide.region_9.10_spmd.clone.sunk | while | flops 131075 | bytes 655516 | solution.py:71
  405.7 6.6 bitcast_add_fusion.10
  430.8 5.0 all-to-all-start.7
  452.4 10.1 all-to-all-done.7
  469.5 4.8 multiply_reduce_fusion.12
  478.0 4.4 all-to-all-start.8
  483.1 22.5 %while.96 = (s32[]{:T(128)}, f32[1,4,64,128]{3,2,1,0:T(8,128)S(1)}, f32[8,1,4,64,128]{4,3,2,1,0:T(8,128)S(1)}, f32[8,1,4,1,1]{2,4,3,1,0:T(1,128)}, f32[8,1,4]{2,...) while((s32[]{:T(128)}, f32[1,4,64,128]{3,2,1,0:T(8,128)S(1)}, ...), condition=%wide.region_15.17_spmd.clone, body=%wide.region_14.16_spmd.clone.sunk | while | flops 131075 | bytes 656552 | solution.py:71
  516.8 13.4 fusion.53
  537.4 19.3 %while.97 = (s32[]{:T(128)}, f32[1,4,64,128]{3,2,1,0:T(8,128)S(1)}, f32[8,1,4,64,128]{4,3,2,1,0:T(8,128)}, f32[8,1,4]{2,1,0:T(1,128)S(1)}, f32[8,1,4,64,128]{4,3...) while((s32[]{:T(128)}, f32[1,4,64,128]{3,2,1,0:T(8,128)S(1)}, ...), condition=%wide.region_19.21_spmd.clone, body=%wide.region_17.20_spmd.clone.sunk | while | flops 196608 | bytes 787668 | solution.py:71
  567.4 10.3 reduce-window.50
  577.8 6.3 fusion.171
  613.6 8.4 bitcast_add_fusion.9
  624.8 10.4 bitcast_add_fusion.8
  640.5 4.7 multiply_reduce_fusion.14
  646.3 6.3 multiply_reduce_fusion.6
  655.2 7.0 fusion.114
  666.0 5.3 all-to-all-start.10
  673.5 30.9 %all-to-all-done.10 = bf16[8,256,256]{1,2,0:T(8,128)(2,1)S(1)} async-done(((bf16[8,256,256]{1,2,0:T(8,128)(2,1)}), bf16[8,256,256]{1,2,0:T(8,128)(2,1)S(1)}, u32[]{:S(2)}, u32[]{:S(2)}) %all-to-all-start.10) | async-done | bytes 1048608 | tf_op jit(solution)/shard_map/all_to_all | solution.py:210
  725.5 9.7 all-to-all-done.9
  735.3 8.0 multiply_reduce_fusion.22
  751.0 4.7 all-to-all-start.12
  756.8 23.6 %while.98 = (s32[]{:T(128)}, f32[1,4,64,128]{3,2,1,0:T(8,128)S(1)}, f32[8,1,4,64,128]{4,3,2,1,0:T(8,128)}, f32[8,1,4,1,1]{2,4,3,1,0:T(1,128)S(1)}, f32[8,1,4]{2,...) while((s32[]{:T(128)}, f32[1,4,64,128]{3,2,1,0:T(8,128)S(1)}, ...), condition=%wide.region_34.36_spmd.clone, body=%wide.region_33.35_spmd.clone.sunk | while | flops 131075 | bytes 656056 | solution.py:71
  789.9 13.8 fusion.55
  810.7 19.4 %while.99 = (s32[]{:T(128)}, f32[1,4,64,128]{3,2,1,0:T(8,128)S(1)}, f32[8,1,4,64,128]{4,3,2,1,0:T(8,128)}, f32[8,1,4]{2,1,0:T(1,128)S(1)}, f32[8,1,4,64,128]{4,3...) while((s32[]{:T(128)}, f32[1,4,64,128]{3,2,1,0:T(8,128)S(1)}, ...), condition=%wide.region_38.40_spmd.clone, body=%wide.region_36.39_spmd.clone.sunk | while | flops 196608 | bytes 787668 | solution.py:71
  840.7 10.1 reduce-window.56
  851.0 6.3 fusion.177
  885.8 8.4 bitcast_add_fusion.7
  897.0 10.6 bitcast_add_fusion.6
  918.7 5.6 multiply_reduce_fusion.10
  927.1 7.0 fusion.115
  937.9 5.3 all-to-all-start.14
  945.5 31.8 %all-to-all-done.14 = bf16[8,256,256]{1,2,0:T(8,128)(2,1)} async-done(((bf16[8,256,256]{1,2,0:T(8,128)(2,1)}), bf16[8,256,256]{1,2,0:T(8,128)(2,1)}, u32[]{:S(2)}, u32[]{:S(2)}) %all-to-all-start.14) | async-done | bytes 1048608 | tf_op jit(solution)/shard_map/all_to_all | solution.py:210
  977.3 4.3 all-to-all-start.13
  981.7 4.7 convert_bitcast_fusion
  987.7 4.9 convert_bitcast_fusion.1
  992.6 15.5 all-to-all-done.13
  1008.1 8.3 multiply_reduce_fusion.23
  1017.4 7.5 pad_maximum_fusion.1
  1025.9 4.6 fusion.45
  1030.5 7.7 fusion.44
  1038.2 11.5 pad_maximum_fusion
  1058.8 72.2 %reduce-scatter.32.cloned.1.call-done = bf16[2,512,1024]{2,1,0:T(8,128)(2,1)} async-done(((bf16[2,2048,1024]{2,1,0:T(8,128)(2,1)}), bf16[2,512,1024]{2,1,0:T(8,128)(2,1)}) %reduce-scatter.32.cloned.1.call-update) | async-done | bytes 2097168 | tf_op jit(solution)/shard_map/reduce_scatter | solution.py:284
  1131.1 166.3 %reduce-scatter.30.cloned.1.call-done = bf16[2,256,4384]{1,2,0:T(8,128)(2,1)} async-done(((bf16[2,1024,4384]{1,2,0:T(8,128)(2,1)}), bf16[2,256,4384]{1,2,0:T(8,128)(2,1)}) %reduce-scatter.30.cloned.1.call-update) | async-done | bytes 4489232 | tf_op jit(solution)/shard_map/reduce_scatter | solution.py:272
  1297.4 12.5 copy.1284
  1312.5 4.8 fusion.189
  1317.5 12.8 reduce-scatter.46.cloned.1.call-done
  1331.9 9.9 all-reduce.35
  1343.5 13.1 reduce-scatter.42.cloned.1.call-done
  1357.6 27.8 %reduce-scatter.40.cloned.1.call-done = bf16[576,8]{1,0:T(8,128)(2,1)} async-done(((bf16[2304,8]{1,0:T(8,128)(2,1)}), bf16[576,8]{1,0:T(8,128)(2,1)}) %reduce-scatter.40.cloned.1.call-update) | async-done | bytes 9232
  1386.6 28.3 %all-reduce.37 = (bf16[2,4,576]{2,1,0:T(4,128)(2,1)S(1)}, bf16[2,576]{1,0:T(2,128)(2,1)S(1)}) all-reduce(bf16[2,4,576]{2,1,0:T(4,128)(2,1)S(1)} %copy.1345, bf16[2,576]{1,0:T(2,128)(2,1)S(1)} %copy.1349), channel_id=19, replica_groups=mesh['batch'=4,'seq'=8] {'seq'}, use_global_device_ids=true, to_apply=%region_65.67.clone | all-reduce | flops 5760 | bytes 23040
  1420.4 34.2 %reduce-scatter.34.cloned.1.call-done = bf16[2,64,1024]{2,1,0:T(8,128)(2,1)} async-done(((bf16[2,512,1024]{2,1,0:T(8,128)(2,1)}), bf16[2,64,1024]{2,1,0:T(8,128)(2,1)}) %reduce-scatter.34.cloned.1.call-update) | async-done | bytes 262160 | tf_op jit(solution)/shard_map/reduce_scatter | solution.py:304
  1456.4 102.7 %all-reduce.40.cloned.1.call-done = bf16[2,256,4384]{2,0,1:T(2,128)(2,1)} async-done(((bf16[2,256,4384]{2,0,1:T(2,128)(2,1)}), bf16[2,256,4384]{2,0,1:T(2,128)(2,1)}) %all-reduce.40.cloned.1.call-update) | async-done | bytes 4489232
  (976 shorter events, 517.2 us)
Async XLA Ops:
  7.2 49.0 %copy-start.31 = (f32[256,1024]{1,0:T(8,128)S(1)}, f32[256,1024]{1,0:T(8,128)}, u32[]{:S(2)}) copy-start(f32[256,1024]{1,0:T(8,128)} %param.24) | copy-start | bytes 3145732
  7.2 87.5 %all-gather.21.cloned.1.call-start = ((), (), s32[]{:S(2)}) async-start(), calls=%async_computation.34 | async-start | bytes 9461760 | tf_op jit(solution)/shard_map/all_gather | solution.py:126
  9.2 168.7 %all-gather.17.cloned.1.call-start = ((), (), s32[]{:S(2)}) async-start(), calls=%async_computation.27 | async-start | bytes 1179648 | tf_op jit(solution)/shard_map/all_gather | solution.py:144
  56.2 45.9 %copy-start.116 = (f32[1024]{0:T(1024)}, f32[1024]{0:T(1024)S(1)}, u32[]{:S(2)}) copy-start(f32[1024]{0:T(1024)S(1)} %convert_element_type.624) | copy-start | bytes 12292
  56.9 45.2 %copy-start.150 = (f32[256]{0:T(256)}, f32[256]{0:T(256)S(1)}, u32[]{:S(2)}) copy-start(f32[256]{0:T(256)S(1)} %fusion.274) | copy-start | bytes 3076
  56.9 47.3 %copy-start.75 = (bf16[2,64,1024]{2,1,0:T(8,128)(2,1)S(1)}, bf16[2,64,1024]{2,1,0:T(8,128)(2,1)}, u32[]{:S(2)}) copy-start(bf16[2,64,1024]{2,1,0:T(8,128)(2,1)} %param.34) | copy-start | bytes 786436
  56.9 48.1 %copy-start.161 = (bf16[2,4,72]{2,1,0:T(4,128)(2,1)S(1)}, bf16[2,4,72]{2,1,0:T(4,128)(2,1)}, u32[]{:S(2)}) copy-start(bf16[2,4,72]{2,1,0:T(4,128)(2,1)} %param.28) | copy-start | bytes 3460
  56.9 48.9 %copy-start.163 = (f32[2,4]{1,0:T(2,128)S(1)}, f32[2,4]{1,0:T(2,128)}, u32[]{:S(2)}) copy-start(f32[2,4]{1,0:T(2,128)} %param.30) | copy-start | bytes 100
  56.9 48.9 %copy-start.155 = (f32[2,4]{1,0:T(2,128)S(1)}, f32[2,4]{1,0:T(2,128)}, u32[]{:S(2)}) copy-start(f32[2,4]{1,0:T(2,128)} %param.31) | copy-start | bytes 100
  56.9 49.0 %copy-start.164 = (f32[2,4]{1,0:T(2,128)S(1)}, f32[2,4]{1,0:T(2,128)}, u32[]{:S(2)}) copy-start(f32[2,4]{1,0:T(2,128)} %param.32) | copy-start | bytes 100
  104.2 168.0 %all-gather.23.cloned.1.call-start = ((), (), s32[]{:S(2)}) async-start(), calls=%async_computation.35 | async-start | bytes 4325376 | tf_op jit(solution)/shard_map/all_gather | solution.py:130
  105.0 196.5 %all-gather.25.cloned.1.call-start = ((), (), s32[]{:S(2)}) async-start(), calls=%async_computation.36 | async-start | bytes 9461760 | tf_op jit(solution)/shard_map/all_gather | solution.py:126
  105.0 1.2 collective-permute-start.5
  105.4 2.3 collective-permute-start
  105.7 93.8 %copy-start.82 = (pred[256,256]{1,0:T(8,128)(4,1)}, pred[256,256]{1,0:T(8,128)(4,1)S(1)}, u32[]{:S(2)}) copy-start(pred[256,256]{1,0:T(8,128)(4,1)S(1)} %iota_compare_fusion) | copy-start | bytes 196612
  105.9 220.6 %copy-start.147 = (f32[4]{0:T(128)}, f32[4]{0:T(128)S(1)}, u32[]{:S(2)}) copy-start(f32[4]{0:T(128)S(1)} %get-tuple-element.1204) | copy-start | bytes 52
  105.9 220.8 %copy-start.137 = (f32[4]{0:T(128)}, f32[4]{0:T(128)S(1)}, u32[]{:S(2)}) copy-start(f32[4]{0:T(128)S(1)} %get-tuple-element.1206) | copy-start | bytes 52
  106.1 114.4 %copy-start.130 = (f32[256]{0:T(256)}, f32[256]{0:T(256)S(1)}, u32[]{:S(2)}) copy-start(f32[256]{0:T(256)S(1)} %mul.1395) | copy-start | bytes 3076
  106.4 3.6 collective-permute-start.6
  107.8 4.0 collective-permute-start.1
  110.0 4.6 collective-permute-start.7
  111.9 4.7 collective-permute-start.2
  114.7 3.6 collective-permute-start.8
  116.7 3.6 collective-permute-start.3
  118.4 3.7 collective-permute-start.9
  120.4 3.7 collective-permute-start.4
  125.5 8.9 all-to-all-start.1
  134.4 37.9 %all-to-all-start = ((bf16[256,8,256]{0,2,1:T(8,128)(2,1)}), bf16[256,8,256]{0,2,1:T(8,128)(2,1)S(1)}, u32[]{:S(2)}, u32[]{:S(2)}) async-start(bf16[256,8,256]{0,2,1:T(8,128)(2,1)} %bitcast.5), calls=%async_computation | async-start | bytes 2097152 | tf_op jit(solution)/shard_map/all_to_all | solution.py:140
  138.0 42.1 %copy-start.98 = (f32[1,512]{1,0:T(1,128)}, f32[1,512]{1,0:T(1,128)S(1)}, u32[]{:S(2)}) copy-start(f32[1,512]{1,0:T(1,128)S(1)} %get-tuple-element.1190) | copy-start | bytes 6148
  138.0 42.1 %copy-start.100 = (f32[1,512]{1,0:T(1,128)}, f32[1,512]{1,0:T(1,128)S(1)}, u32[]{:S(2)}) copy-start(f32[1,512]{1,0:T(1,128)S(1)} %get-tuple-element.1191) | copy-start | bytes 6148
  138.0 42.1 %copy-start.102 = (f32[1,512]{1,0:T(1,128)}, f32[1,512]{1,0:T(1,128)S(1)}, u32[]{:S(2)}) copy-start(f32[1,512]{1,0:T(1,128)S(1)} %get-tuple-element.1192) | copy-start | bytes 6148
  138.0 42.1 %copy-start.104 = (f32[1,512]{1,0:T(1,128)}, f32[1,512]{1,0:T(1,128)S(1)}, u32[]{:S(2)}) copy-start(f32[1,512]{1,0:T(1,128)S(1)} %get-tuple-element.1193) | copy-start | bytes 6148
  172.3 41.1 %all-to-all-start.2 = ((bf16[256,8,256]{0,2,1:T(8,128)(2,1)}), bf16[256,8,256]{0,2,1:T(8,128)(2,1)}, u32[]{:S(2)}, u32[]{:S(2)}) async-start(bf16[256,8,256]{0,2,1:T(8,128)(2,1)} %bitcast.38), calls=%async_computation.2 | async-start | bytes 2097152 | tf_op jit(solution)/shard_map/all_to_all | solution.py:141
  225.4 42.3 %all-to-all-start.3 = ((bf16[8,256,256]{1,2,0:T(8,128)(2,1)}), bf16[8,256,256]{1,2,0:T(8,128)(2,1)S(1)}, u32[]{:S(2)}, u32[]{:S(2)}) async-start(bf16[8,256,256]{1,2,0:T(8,128)(2,1)} %copy.1153), calls=%async_computation.3 | async-start | bytes 2097152 | tf_op jit(solution)/shard_map/all_to_all | solution.py:170
  229.0 130.9 %all-gather.19.cloned.1.call-start = ((), (), s32[]{:S(2)}) async-start(), calls=%async_computation.28 | async-start | bytes 1179648 | tf_op jit(solution)/shard_map/all_gather | solution.py:144
  229.1 72.4 %copy-start.118 = (f32[1024]{0:T(1024)}, f32[1024]{0:T(1024)S(1)}, u32[]{:S(2)}) copy-start(f32[1024]{0:T(1024)S(1)} %convert_element_type.626) | copy-start | bytes 12292
  310.9 158.6 %all-gather.27.cloned.1.call-start = ((), (), s32[]{:S(2)}) async-start(), calls=%async_computation.37 | async-start | bytes 4325376 | tf_op jit(solution)/shard_map/all_gather | solution.py:130
  312.3 162.0 %copy-start.73 = (f32[2048]{0:T(1024)}, f32[2048]{0:T(1024)S(1)}, u32[]{:S(2)}) copy-start(f32[2048]{0:T(1024)S(1)} %convert_element_type.627) | copy-start | bytes 24580
  313.6 9.0 all-to-all-start.5
  322.6 31.9 %all-to-all-start.4 = ((bf16[256,8,256]{0,2,1:T(8,128)(2,1)}), bf16[256,8,256]{0,2,1:T(8,128)(2,1)S(1)}, u32[]{:S(2)}, u32[]{:S(2)}) async-start(bf16[256,8,256]{0,2,1:T(8,128)(2,1)} %bitcast.49), calls=%async_computation.4 | async-start | bytes 2097152 | tf_op jit(solution)/shard_map/all_to_all | solution.py:140
  354.5 63.4 %all-to-all-start.6 = ((bf16[256,8,256]{0,2,1:T(8,128)(2,1)}), bf16[256,8,256]{0,2,1:T(8,128)(2,1)}, u32[]{:S(2)}, u32[]{:S(2)}) async-start(bf16[256,8,256]{0,2,1:T(8,128)(2,1)} %bitcast.82), calls=%async_computation.6 | async-start | bytes 2097152 | tf_op jit(solution)/shard_map/all_to_all | solution.py:141
  374.0 74.8 %copy-start.6 = (f32[32,8,8,256]{3,2,1,0:T(8,128)}, f32[32,8,8,256]{3,2,1,0:T(8,128)S(1)}, u32[]{:S(2)}) copy-start(f32[32,8,8,256]{3,2,1,0:T(8,128)S(1)} %copy.1374) | copy-start | bytes 6291460
  430.8 31.6 %all-to-all-start.7 = ((bf16[8,256,256]{1,2,0:T(8,128)(2,1)}), bf16[8,256,256]{1,2,0:T(8,128)(2,1)}, u32[]{:S(2)}, u32[]{:S(2)}) async-start(bf16[8,256,256]{1,2,0:T(8,128)(2,1)} %copy.1178), calls=%async_computation.7 | async-start | bytes 2097152 | tf_op jit(solution)/shard_map/all_to_all | solution.py:170
  478.0 31.0 %all-to-all-start.8 = ((bf16[256,8,256]{0,2,1:T(8,128)(2,1)}), bf16[256,8,256]{0,2,1:T(8,128)(2,1)}, u32[]{:S(2)}, u32[]{:S(2)}) async-start(bf16[256,8,256]{0,2,1:T(8,128)(2,1)} %bitcast.113), calls=%async_computation.8 | async-start | bytes 2097152 | tf_op jit(solution)/shard_map/all_to_all | solution.py:197
  592.0 73.9 %all-to-all-start.11 = ((bf16[8,256,4]{1,2,0:T(4,128)(2,1)}), bf16[8,256,4]{1,2,0:T(4,128)(2,1)S(1)}, u32[]{:S(2)}, u32[]{:S(2)}) async-start(bf16[8,256,4]{1,2,0:T(4,128)(2,1)} %bitcast.161), calls=%async_computation.12 | async-start | bytes 32768 | tf_op jit(solution)/shard_map/all_to_all | solution.py:224
  666.0 38.5 %all-to-all-start.10 = ((bf16[8,256,256]{1,2,0:T(8,128)(2,1)}), bf16[8,256,256]{1,2,0:T(8,128)(2,1)S(1)}, u32[]{:S(2)}, u32[]{:S(2)}) async-start(bf16[8,256,256]{1,2,0:T(8,128)(2,1)} %bitcast.912), calls=%async_computation.10 | async-start | bytes 2097152 | tf_op jit(solution)/shard_map/all_to_all | solution.py:210
  671.2 64.0 %reduce-scatter.26.cloned.1.call-start = ((), (), s32[]{:S(2)}) async-start(), calls=%async_computation.29 | async-start | bytes 1179648 | tf_op jit(solution)/shard_map/reduce_scatter | solution.py:232
  704.5 30.8 %all-to-all-start.9 = ((bf16[8,256,256]{1,2,0:T(8,128)(2,1)}), bf16[8,256,256]{1,2,0:T(8,128)(2,1)}, u32[]{:S(2)}, u32[]{:S(2)}) async-start(bf16[8,256,256]{1,2,0:T(8,128)(2,1)} %copy.1203), calls=%async_computation.9 | async-start | bytes 2097152 | tf_op jit(solution)/shard_map/all_to_all | solution.py:217
  751.0 31.3 %all-to-all-start.12 = ((bf16[256,8,256]{0,2,1:T(8,128)(2,1)}), bf16[256,8,256]{0,2,1:T(8,128)(2,1)}, u32[]{:S(2)}, u32[]{:S(2)}) async-start(bf16[256,8,256]{0,2,1:T(8,128)(2,1)} %bitcast.990), calls=%async_computation.13 | async-start | bytes 2097152 | tf_op jit(solution)/shard_map/all_to_all | solution.py:197
  864.1 73.8 %all-to-all-start.15 = ((bf16[8,256,4]{1,2,0:T(4,128)(2,1)}), bf16[8,256,4]{1,2,0:T(4,128)(2,1)S(1)}, u32[]{:S(2)}, u32[]{:S(2)}) async-start(bf16[8,256,4]{1,2,0:T(4,128)(2,1)} %bitcast.236), calls=%async_computation.17 | async-start | bytes 32768 | tf_op jit(solution)/shard_map/all_to_all | solution.py:224
  937.9 39.4 %all-to-all-start.14 = ((bf16[8,256,256]{1,2,0:T(8,128)(2,1)}), bf16[8,256,256]{1,2,0:T(8,128)(2,1)}, u32[]{:S(2)}, u32[]{:S(2)}) async-start(bf16[8,256,256]{1,2,0:T(8,128)(2,1)} %bitcast.911), calls=%async_computation.15 | async-start | bytes 2097152 | tf_op jit(solution)/shard_map/all_to_all | solution.py:210
  943.2 64.9 %reduce-scatter.28.cloned.1.call-start = ((), (), s32[]{:S(2)}) async-start(), calls=%async_computation.30 | async-start | bytes 1179648 | tf_op jit(solution)/shard_map/reduce_scatter | solution.py:232
  977.3 30.8 %all-to-all-start.13 = ((bf16[8,256,256]{1,2,0:T(8,128)(2,1)}), bf16[8,256,256]{1,2,0:T(8,128)(2,1)}, u32[]{:S(2)}, u32[]{:S(2)}) async-start(bf16[8,256,256]{1,2,0:T(8,128)(2,1)} %copy.1255), calls=%async_computation.14 | async-start | bytes 2097152 | tf_op jit(solution)/shard_map/all_to_all | solution.py:217
  981.6 69.3 %reduce-scatter.44.cloned.1.call-start = ((), (), s32[]{:S(2)}) async-start(), calls=%async_computation.42 | async-start | bytes 655360
  987.6 70.6 %reduce-scatter.36.cloned.1.call-start = ((), (), s32[]{:S(2)}) async-start(), calls=%async_computation.38 | async-start | bytes 327680
  1017.4 113.7 %reduce-scatter.32.cloned.1.call-start = ((), (), s32[]{:S(2)}) async-start(), calls=%async_computation.32 | async-start | bytes 10485760 | tf_op jit(solution)/shard_map/reduce_scatter | solution.py:284
  1025.0 272.4 %reduce-scatter.30.cloned.1.call-start = ((), (), s32[]{:S(2)}) async-start(), calls=%async_computation.31 | async-start | bytes 22446080 | tf_op jit(solution)/shard_map/reduce_scatter | solution.py:272
  1049.8 280.5 %reduce-scatter.46.cloned.1.call-start = ((), (), s32[]{:S(2)}) async-start(), calls=%async_computation.43 | async-start | bytes 147456
  1050.9 305.8 %reduce-scatter.42.cloned.1.call-start = ((), (), s32[]{:S(2)}) async-start(), calls=%async_computation.41 | async-start | bytes 737280
  1052.5 332.9 %reduce-scatter.40.cloned.1.call-start = ((), (), s32[]{:S(2)}) async-start(), calls=%async_computation.40 | async-start | bytes 737280
  1058.2 360.8 %reduce-scatter.38.cloned.1.call-start = ((), (), s32[]{:S(2)}) async-start(), calls=%async_computation.39 | async-start | bytes 73728
  1058.8 395.8 %reduce-scatter.34.cloned.1.call-start = ((), (), s32[]{:S(2)}) async-start(), calls=%async_computation.33 | async-start | bytes 2359296 | tf_op jit(solution)/shard_map/reduce_scatter | solution.py:304
  1131.1 428.0 %all-reduce.40.cloned.1.call-start = ((), (), s32[]{:S(2)}) async-start(), calls=%async_computation.44 | async-start | bytes 9175040
  1312.5 103.7 %copy-start.125 = (f32[256]{0:T(256)S(1)}, f32[256]{0:T(256)}, u32[]{:S(2)}) copy-start(f32[256]{0:T(256)} %copy-done.124) | copy-start | bytes 3076
  (148 other events, 1160.4 us)
Sparse Core Ops, SparseCore 0:
  11.4 83.2 all-gather.20
  104.3 22.6 all-gather.16
  129.9 71.8 all-gather.22
  204.5 96.8 all-gather.24
  311.0 25.3 all-gather.18
  339.3 69.7 all-gather.26
  674.9 35.1 reduce-scatter.25
  946.3 35.0 reduce-scatter.27
  987.7 26.3 reduce-scatter.43
  1017.5 24.0 reduce-scatter.35
  1044.7 86.2 reduce-scatter.31
  1134.1 163.2 reduce-scatter.29
  1299.6 30.5 reduce-scatter.45
  1333.0 23.6 reduce-scatter.41
  1359.9 25.4 reduce-scatter.39
  1387.5 30.5 reduce-scatter.37
  1420.2 34.3 reduce-scatter.33
  1456.8 102.2 all-reduce.39
